TPU v7x, 32 devices: a whole 2x2x4 slice. The times are simulated.
32 devices in a mesh: mem: 8 (over y, x, core), lat: 4 (over z).
Axes of the slice: x: 2, y: 2, z: 4, core: 2. Of those that a mesh axis runs over, the one named last changes fastest.
Arguments:
- coarse_weights: bfloat16 [32, 32, 8, 128], P('lat', 'mem'), may hold values from -6 to 6
- perturbations: bfloat16 [32, 8, 128, 512], P('mem', None, 'lat'), may hold values from -6 to 6
- lat_matrix: bfloat16 [128, 32], P('lat'), may hold values from -1 to 1
- lon_matrix: bfloat16 [128, 512], replicated, may hold values from -0.5 to 0.5
- wind_field: float32 [2, 128, 512], P(None, 'lat', 'mem'), may hold values from -0.4 to 0.4
- observed_cell: int32 [4, 8, 128, 64], P(None, None, 'lat', 'mem'), may hold values from 0 to 7
- observed_value: float32 [4, 8, 128, 64], P(None, None, 'lat', 'mem'), may hold values from -6 to 6
- observed_weight: float32 [4, 8, 128, 64], P(None, None, 'lat', 'mem'), may hold values from 0.5 to 4
Outputs:
- gradient: float32 [32, 32, 8, 128], P('lat', 'mem')
- increment: float32 [8, 128, 512], P(None, 'lat', 'mem')
Inputs may be any that keep to these rules, and one draw needn't show every extreme that they name: `observed_cell`: the observed cell is an offset within its block of 8 longitudes.
All inputs are finite; a program needn't handle non-finite values.
Results may differ from a plain program's by a relative error of at most 0.0003.
Values may be sent and summed in bfloat16 or wider, within the bound.
A program may use at most 64 MiB of HBM per device.

v0:
```python
import jax
import jax.numpy as jnp
from jax import lax
from jax.sharding import PartitionSpec as P

STEPS = 4
OBLK = 8
diffusion = 0.2
highest = lax.Precision.HIGHEST


def padded_2(value, sides, width):
    for axis, dim in sides:
        peers, length = (lax.axis_size(axis), value.shape[dim])
        up = [(i, (i + 1) % peers) for i in range(peers - 1)]
        down = [(j, i) for i, j in up]
        last = lax.slice_in_dim(value, length - width, length, axis=dim)
        initial = lax.slice_in_dim(value, 0, width, axis=dim)
        before = lax.ppermute(last, axis, up)
        after = lax.ppermute(initial, axis, down)
        value = jnp.concatenate([before, value, after], axis=dim)
    return value


def stencil_parts(padded):
    center = padded[:, 1:-1, 1:-1]
    north_cell = padded[:, 2:, 1:-1]
    south_cell = padded[:, :-2, 1:-1]
    east_cell = padded[:, 1:-1, 2:]
    west_cell = padded[:, 1:-1, :-2]
    return (center, north_cell, south_cell, east_cell, west_cell)


def advance(padded, wind_out):
    center, north_cell, south_cell, east_cell, west_cell = stencil_parts(padded)
    spread = north_cell + south_cell + east_cell + west_cell - 4.0 * center
    return (
        center
        + diffusion * spread
        - 0.5 * wind_out[1] * (north_cell - south_cell)
        - 0.5 * wind_out[0] * (east_cell - west_cell)
    )


def retreat(padded, wind_in):
    center, north_cell, south_cell, east_cell, west_cell = stencil_parts(padded)
    spread = north_cell + south_cell + east_cell + west_cell - 4.0 * center
    along_lon = wind_in[0] * padded
    along_lat = wind_in[1] * padded
    return (
        center
        + diffusion * spread
        + 0.5 * (along_lat[:, 2:, 1:-1] - along_lat[:, :-2, 1:-1])
        + 0.5 * (along_lon[:, 1:-1, 2:] - along_lon[:, 1:-1, :-2])
    )


def observe(tangent, picked, observed, weighting):
    levels, row_count, col_count = tangent.shape
    blocks = tangent.reshape(levels, row_count, col_count // OBLK, OBLK)
    onehot = (picked[..., None] == jnp.arange(OBLK, dtype=jnp.int32)).astype(jnp.float32)
    looked = jnp.sum(blocks * onehot, axis=-1)
    misfit = weighting * (looked - observed)
    return (misfit[..., None] * onehot).reshape(levels, row_count, col_count)


def domain_mask(margin, row_count, col_count):
    lat_start = lax.axis_index("lat") * row_count - margin
    lon_start = lax.axis_index("mem") * col_count - margin
    row_place = lat_start + jnp.arange(row_count + 2 * margin, dtype=jnp.int32)
    col_place = lon_start + jnp.arange(col_count + 2 * margin, dtype=jnp.int32)
    rows_inside = (row_place >= 0) & (row_place < row_count * lax.axis_size("lat"))
    cols_inside = (col_place >= 0) & (col_place < col_count * lax.axis_size("mem"))
    return (rows_inside[:, None] & cols_inside[None, :]).astype(jnp.float32)


def body(
    coarse_weights,
    perturbations,
    lat_matrix,
    lon_matrix,
    wind_field,
    observed_cell,
    observed_value,
    observed_weight,
):
    members_here, levels, row_count, lon_total = perturbations.shape
    col_count = wind_field.shape[2]
    members_all = members_here * lax.axis_size("mem")
    member_scale = 1.0 / jnp.sqrt(jnp.float32(members_all - 1))
    lat_full = lat_matrix.astype(jnp.float32)
    lon_full = lon_matrix.astype(jnp.float32)
    widened = jnp.einsum(
        "cmlw,wf->cmlf", coarse_weights.astype(jnp.float32), lon_full, precision=highest
    )
    columns = lat_full
    localized = jnp.einsum(
        "rc,cmlf->mlrf",
        columns,
        lax.all_gather(widened, "lat", axis=0, tiled=True),
        precision=highest,
    )
    partial_sum = jnp.sum(localized * perturbations, axis=0)
    increment = lax.psum_scatter(partial_sum, "mem", scatter_dimension=2, tiled=True) * member_scale
    wide_wind = padded_2(wind_field, (("mem", 2), ("lat", 1)), STEPS)

    def wind_margin(margin):
        return wide_wind[
            :,
            STEPS - margin : STEPS + row_count + margin,
            STEPS - margin : STEPS + col_count + margin,
        ]

    forcings = []
    tangent = padded_2(increment, (("mem", 2), ("lat", 1)), STEPS)
    for step_index in range(STEPS):
        margin = STEPS - step_index - 1
        tangent = advance(tangent, wind_margin(margin)) * domain_mask(margin, row_count, col_count)
        inner = tangent[:, margin : margin + row_count, margin : margin + col_count]
        forcings.append(
            observe(
                inner,
                observed_cell[step_index],
                observed_value[step_index],
                observed_weight[step_index],
            )
        )
    adjoint = jnp.zeros_like(increment)
    for step_index in reversed(range(STEPS)):
        padded = padded_2(adjoint + forcings[step_index], (("mem", 2), ("lat", 1)), 1)
        adjoint = retreat(padded, wind_margin(1))
    product = perturbations * lax.all_gather(adjoint, "mem", axis=2, tiled=True)[None]
    projected = jnp.einsum("mlrf,wf->mlrw", product, lon_full, precision=highest)
    columns = lat_full
    banded = lax.psum_scatter(
        jnp.einsum("rc,mlrw->cmlw", columns, projected, precision=highest),
        "lat",
        scatter_dimension=0,
        tiled=True,
    )
    gradient = banded * member_scale + coarse_weights.astype(jnp.float32)
    return (gradient, increment)


def solution(mesh):
    in_specs = (
        P("lat", "mem", None, None),
        P("mem", None, "lat", None),
        P("lat", None),
        P(),
        P(None, "lat", "mem"),
        P(None, None, "lat", "mem"),
        P(None, None, "lat", "mem"),
        P(None, None, "lat", "mem"),
    )
    out_specs = (P("lat", "mem", None, None), P(None, "lat", "mem"))
    return jax.shard_map(body, mesh=mesh, in_specs=in_specs, out_specs=out_specs, check_vma=False)
```

profile of v0, /device:TPU:0, one launch (start us, length us, event | category | flops | bytes accessed | tf_op | source)
XLA Modules:
  0.0 257.9 jit_solution(16076721269377844049)
XLA Ops:
  8.1 1.9 fusion.53
  11.5 2.4 collective-permute-start.4
  19.0 39.5 %all-gather.2.cloned.1.call-done = f32[32,4,8,512]{3,0,2,1:T(8,128)} async-done(((f32[8,4,8,512]{3,0,2,1:T(8,128)}), f32[32,4,8,512]{3,0,2,1:T(8,128)}) %all-gather.2.cloned.1.call-update) | async-done | bytes 2097168 | tf_op jit(solution)/shard_map/all_gather | solution.py:100
  58.5 3.7 %fusion = f32[8,32,512]{2,1,0:T(8,128)} fusion(bf16[4,8,32,512]{3,2,1,0:T(8,128)(2,1)S(1)} %copy-done.1, f32[32,4,8,512]{3,0,2,1:T(8,128)} %all-gather.2.cloned.1.call-done, bf16[32,32]{1,0:T(8,128)(2,1)} %param.10), kind=kOutput, calls=%fused_computation.2 | convolution fusion | flops 202768384 | bytes 3672064 | tf_op jit(solution)/shard_map/rc,cmlf->mlrf/dot_general | solution.py:97
  62.2 1.8 copy.254
  65.7 2.1 collective-permute-start.6
  69.4 3.9 %collective-permute-done.7 = f32[2,4,72]{2,1,0:T(4,128)S(1)} collective-permute-done((f32[2,4,72]{2,1,0:T(4,128)S(1)}, f32[2,4,72]{2,1,0:T(4,128)S(1)}, u32[]{:S(2)}, u32[]{:S(2)}) %collective-permute-start.7) | collective-permute-done | bytes 2336 | tf_op jit(solution)/shard_map/ppermute | solution.py:20
  74.2 24.3 %reduce-scatter.7.cloned.1.call-done = f32[64,256]{1,0:T(8,128)} async-done(((f32[512,256]{1,0:T(8,128)}), f32[64,256]{1,0:T(8,128)}) %reduce-scatter.7.cloned.1.call-update) | async-done | bytes 65552
  102.5 3.5 %collective-permute-done.1 = f32[8,32,4]{2,1,0:T(8,128)S(1)} collective-permute-done((f32[8,32,4]{2,1,0:T(8,128)S(1)}, f32[8,32,4]{2,1,0:T(8,128)S(1)}, u32[]{:S(2)}, u32[]{:S(2)}) %collective-permute-start.1) | collective-permute-done | bytes 4128 | tf_op jit(solution)/shard_map/ppermute | solution.py:20
  106.3 3.4 %collective-permute-start.2 = (f32[8,4,72]{1,2,0:T(8,128)S(1)}, f32[8,4,72]{1,2,0:T(8,128)S(1)}, u32[]{:S(2)}, u32[]{:S(2)}) collective-permute-start(f32[8,4,72]{1,2,0:T(8,128)S(1)} %copy.233), channel_id=1, source_target_pairs={{0,1},{1,2},{2,3},{4,5},{5,6},{6,7},{8,9},{9,10},{10,11},{12,13},{... | collective-permute-start | bytes 27656 | tf_op jit(solution)/shard_map/ppermute | solution.py:19
  112.1 2.5 collective-permute-done.2
  114.6 4.9 %collective-permute-done.3 = f32[8,4,72]{1,2,0:T(8,128)S(1)} collective-permute-done((f32[8,4,72]{1,2,0:T(8,128)S(1)}, f32[8,4,72]{1,2,0:T(8,128)S(1)}, u32[]{:S(2)}, u32[]{:S(2)}) %collective-permute-start.3) | collective-permute-done | bytes 9248 | tf_op jit(solution)/shard_map/ppermute | solution.py:20
  121.7 4.0 %collective-permute-start.8 = (f32[8,32,1]{1,2,0:T(1,128)S(1)}, f32[8,32,1]{1,2,0:T(1,128)S(1)}, u32[]{:S(2)}, u32[]{:S(2)}) collective-permute-start(f32[8,32,1]{1,2,0:T(1,128)S(1)} %get-tuple-element.40), channel_id=1, source_target_pairs={{0,4},{4,8},{8,12},{12,16},{16,20},{20,24},{24,28},{1,5},{5,9},{9,... | collective-permute-start | bytes 3080 | tf_op jit(solution)/shard_map/ppermute | solution.py:19
  127.1 3.5 %collective-permute-done.9 = f32[8,32,1]{1,2,0:T(1,128)S(1)} collective-permute-done((f32[8,32,1]{1,2,0:T(1,128)S(1)}, f32[8,32,1]{1,2,0:T(1,128)S(1)}, u32[]{:S(2)}, u32[]{:S(2)}) %collective-permute-start.9) | collective-permute-done | bytes 1056 | tf_op jit(solution)/shard_map/ppermute | solution.py:20
  132.1 4.6 %collective-permute-start.11 = (f32[8,1,66]{1,2,0:T(8,128)S(1)}, f32[8,1,66]{1,2,0:T(8,128)S(1)}, u32[]{:S(2)}, u32[]{:S(2)}) collective-permute-start(f32[8,1,66]{1,2,0:T(8,128)S(1)} %get-tuple-element.28), channel_id=1, source_target_pairs={{0,1},{1,2},{2,3},{4,5},{5,6},{6,7},{8,9},{9,10},{10,11},{12,13},{... | collective-permute-start | bytes 6344 | tf_op jit(solution)/shard_map/ppermute | solution.py:19
  136.8 4.3 %collective-permute-done.10 = f32[8,1,66]{1,2,0:T(8,128)S(1)} collective-permute-done((f32[8,1,66]{1,2,0:T(8,128)S(1)}, f32[8,1,66]{1,2,0:T(8,128)S(1)}, u32[]{:S(2)}, u32[]{:S(2)}) %collective-permute-start.10) | collective-permute-done | bytes 2144 | tf_op jit(solution)/shard_map/ppermute | solution.py:20
  141.1 1.7 collective-permute-done.11
  143.7 3.1 %collective-permute-start.12 = (f32[8,32,1]{1,2,0:T(1,128)S(1)}, f32[8,32,1]{1,2,0:T(1,128)S(1)}, u32[]{:S(2)}, u32[]{:S(2)}) collective-permute-start(f32[8,32,1]{1,2,0:T(1,128)S(1)} %get-tuple-element.38), channel_id=1, source_target_pairs={{0,4},{4,8},{8,12},{12,16},{16,20},{20,24},{24,28},{1,5},{5,9},{9,... | collective-permute-start | bytes 3080 | tf_op jit(solution)/shard_map/ppermute | solution.py:19
  148.1 1.8 collective-permute-done.13
  151.4 4.9 %collective-permute-start.15 = (f32[8,1,66]{1,2,0:T(8,128)S(1)}, f32[8,1,66]{1,2,0:T(8,128)S(1)}, u32[]{:S(2)}, u32[]{:S(2)}) collective-permute-start(f32[8,1,66]{1,2,0:T(8,128)S(1)} %get-tuple-element.26), channel_id=1, source_target_pairs={{0,1},{1,2},{2,3},{4,5},{5,6},{6,7},{8,9},{9,10},{10,11},{12,13},{... | collective-permute-start | bytes 6344 | tf_op jit(solution)/shard_map/ppermute | solution.py:19
  156.3 4.1 %collective-permute-done.14 = f32[8,1,66]{1,2,0:T(8,128)S(1)} collective-permute-done((f32[8,1,66]{1,2,0:T(8,128)S(1)}, f32[8,1,66]{1,2,0:T(8,128)S(1)}, u32[]{:S(2)}, u32[]{:S(2)}) %collective-permute-start.14) | collective-permute-done | bytes 2144 | tf_op jit(solution)/shard_map/ppermute | solution.py:20
  162.9 3.5 %collective-permute-start.16 = (f32[8,32,1]{1,2,0:T(1,128)S(1)}, f32[8,32,1]{1,2,0:T(1,128)S(1)}, u32[]{:S(2)}, u32[]{:S(2)}) collective-permute-start(f32[8,32,1]{1,2,0:T(1,128)S(1)} %get-tuple-element.36), channel_id=1, source_target_pairs={{0,4},{4,8},{8,12},{12,16},{16,20},{20,24},{24,28},{1,5},{5,9},{9,... | collective-permute-start | bytes 3080 | tf_op jit(solution)/shard_map/ppermute | solution.py:19
  167.8 1.8 collective-permute-done.17
  171.0 5.0 %collective-permute-start.19 = (f32[8,1,66]{1,2,0:T(8,128)S(1)}, f32[8,1,66]{1,2,0:T(8,128)S(1)}, u32[]{:S(2)}, u32[]{:S(2)}) collective-permute-start(f32[8,1,66]{1,2,0:T(8,128)S(1)} %get-tuple-element.24), channel_id=1, source_target_pairs={{0,1},{1,2},{2,3},{4,5},{5,6},{6,7},{8,9},{9,10},{10,11},{12,13},{... | collective-permute-start | bytes 6344 | tf_op jit(solution)/shard_map/ppermute | solution.py:19
  176.0 4.2 %collective-permute-done.18 = f32[8,1,66]{1,2,0:T(8,128)S(1)} collective-permute-done((f32[8,1,66]{1,2,0:T(8,128)S(1)}, f32[8,1,66]{1,2,0:T(8,128)S(1)}, u32[]{:S(2)}, u32[]{:S(2)}) %collective-permute-start.18) | collective-permute-done | bytes 2144 | tf_op jit(solution)/shard_map/ppermute | solution.py:20
  182.7 3.5 %collective-permute-start.20 = (f32[8,32,1]{1,2,0:T(1,128)S(1)}, f32[8,32,1]{1,2,0:T(1,128)S(1)}, u32[]{:S(2)}, u32[]{:S(2)}) collective-permute-start(f32[8,32,1]{1,2,0:T(1,128)S(1)} %get-tuple-element.30), channel_id=1, source_target_pairs={{0,4},{4,8},{8,12},{12,16},{16,20},{20,24},{24,28},{1,5},{5,9},{9,... | collective-permute-start | bytes 3080 | tf_op jit(solution)/shard_map/ppermute | solution.py:19
  187.5 2.0 collective-permute-done.21
  190.9 5.0 %collective-permute-start.23 = (f32[8,1,66]{1,2,0:T(8,128)S(1)}, f32[8,1,66]{1,2,0:T(8,128)S(1)}, u32[]{:S(2)}, u32[]{:S(2)}) collective-permute-start(f32[8,1,66]{1,2,0:T(8,128)S(1)} %get-tuple-element.22), channel_id=1, source_target_pairs={{0,1},{1,2},{2,3},{4,5},{5,6},{6,7},{8,9},{9,10},{10,11},{12,13},{... | collective-permute-start | bytes 6344 | tf_op jit(solution)/shard_map/ppermute | solution.py:19
  196.0 4.2 %collective-permute-done.22 = f32[8,1,66]{1,2,0:T(8,128)S(1)} collective-permute-done((f32[8,1,66]{1,2,0:T(8,128)S(1)}, f32[8,1,66]{1,2,0:T(8,128)S(1)}, u32[]{:S(2)}, u32[]{:S(2)}) %collective-permute-start.22) | collective-permute-done | bytes 2144 | tf_op jit(solution)/shard_map/ppermute | solution.py:20
  202.7 17.4 %all_gather.7 = f32[8,32,512]{1,2,0:T(8,128)S(1)} all-gather(f32[8,32,64]{1,2,0:T(8,128)S(1)} %fusion.4), channel_id=1, replica_groups=mesh['mem'=8,'lat'=4] {'mem'}, dimensions={2}, use_global_device_ids=true | all-gather | bytes 589824 | tf_op jit(solution)/shard_map/all_gather | solution.py:132
  221.5 2.2 fusion.1
  225.0 24.8 %reduce-scatter.5.cloned.1.call-done = f32[8,4,8,128]{3,0,2,1:T(8,128)} async-done(((f32[32,4,8,128]{3,0,2,1:T(8,128)}), f32[8,4,8,128]{3,0,2,1:T(8,128)}) %reduce-scatter.5.cloned.1.call-update) | async-done | bytes 131088 | tf_op jit(solution)/shard_map/reduce_scatter | solution.py:135
  (130 shorter events, 44.0 us)
Async XLA Ops:
  7.2 51.3 %copy-start.1 = (bf16[4,8,32,512]{3,2,1,0:T(8,128)(2,1)S(1)}, bf16[4,8,32,512]{3,2,1,0:T(8,128)(2,1)}, u32[]{:S(2)}) copy-start(bf16[4,8,32,512]{3,2,1,0:T(8,128)(2,1)} %param.9) | copy-start | bytes 3145732
  7.2 51.3 %all-gather.2.cloned.1.call-start = ((), (), s32[]{:S(2)}) async-start(), calls=%async_computation.2 | async-start | bytes 2621440 | tf_op jit(solution)/shard_map/all_gather | solution.py:100
  10.0 88.6 %reduce-scatter.7.cloned.1.call-start = ((), (), s32[]{:S(2)}) async-start(), calls=%async_computation.4 | async-start | bytes 589824
  11.5 54.0 %collective-permute-start.4 = (f32[2,32,4]{2,1,0:T(8,128)}, f32[2,32,4]{2,1,0:T(8,128)S(1)}, u32[]{:S(2)}, u32[]{:S(2)}) collective-permute-start(f32[2,32,4]{2,1,0:T(8,128)} %get-tuple-element.62), channel_id=1, source_target_pairs={{0,4},{4,8},{8,12},{12,16},{16,20},{20,24},{24,28},{1,5},{5,9},{9,... | collective-permute-start | bytes 3080 | tf_op jit(solution)/shard_map/ppermute | solution.py:19
  13.9 51.6 %collective-permute-start.5 = (f32[2,32,4]{2,1,0:T(8,128)}, f32[2,32,4]{2,1,0:T(8,128)S(1)}, u32[]{:S(2)}, u32[]{:S(2)}) collective-permute-start(f32[2,32,4]{2,1,0:T(8,128)} %get-tuple-element.63), channel_id=1, source_target_pairs={{4,0},{8,4},{12,8},{16,12},{20,16},{24,20},{28,24},{5,1},{9,5},{13... | collective-permute-start | bytes 3080 | tf_op jit(solution)/shard_map/ppermute | solution.py:20
  65.5 184.3 %reduce-scatter.5.cloned.1.call-start = ((), (), s32[]{:S(2)}) async-start(), calls=%async_computation.3 | async-start | bytes 655360 | tf_op jit(solution)/shard_map/reduce_scatter | solution.py:135
  65.7 3.7 %collective-permute-start.6 = (f32[2,4,72]{2,1,0:T(4,128)S(1)}, f32[2,4,72]{2,1,0:T(4,128)S(1)}, u32[]{:S(2)}, u32[]{:S(2)}) collective-permute-start(f32[2,4,72]{2,1,0:T(4,128)S(1)} %get-tuple-element.50), channel_id=1, source_target_pairs={{0,1},{1,2},{2,3},{4,5},{5,6},{6,7},{8,9},{9,10},{10,11},{12,13},{... | collective-permute-start | bytes 6920 | tf_op jit(solution)/shard_map/ppermute | solution.py:19
  67.8 5.5 %collective-permute-start.7 = (f32[2,4,72]{2,1,0:T(4,128)S(1)}, f32[2,4,72]{2,1,0:T(4,128)S(1)}, u32[]{:S(2)}, u32[]{:S(2)}) collective-permute-start(f32[2,4,72]{2,1,0:T(4,128)S(1)} %get-tuple-element.51), channel_id=1, source_target_pairs={{1,0},{2,1},{3,2},{5,4},{6,5},{7,6},{9,8},{10,9},{11,10},{13,12},{... | collective-permute-start | bytes 6920 | tf_op jit(solution)/shard_map/ppermute | solution.py:20
  99.6 20.0 %copy-start.7 = (f32[38,70]{0,1:T(8,128)S(1)}, f32[38,70]{0,1:T(8,128)}, u32[]{:S(2)}) copy-start(f32[38,70]{0,1:T(8,128)} %and_convert_fusion.2) | copy-start | bytes 31924
  99.7 20.4 %copy-start.2 = (f32[8,32,64]{2,1,0:T(8,128)}, f32[8,32,64]{2,1,0:T(8,128)S(1)}, u32[]{:S(2)}) copy-start(f32[8,32,64]{2,1,0:T(8,128)S(1)} %broadcast_multiply_fusion.8) | copy-start | bytes 196612
  99.8 2.7 %collective-permute-start = (f32[8,32,4]{2,1,0:T(8,128)S(1)}, f32[8,32,4]{2,1,0:T(8,128)S(1)}, u32[]{:S(2)}, u32[]{:S(2)}) collective-permute-start(f32[8,32,4]{2,1,0:T(8,128)S(1)} %get-tuple-element.48), channel_id=1, source_target_pairs={{0,4},{4,8},{8,12},{12,16},{16,20},{20,24},{24,28},{1,5},{5,9},{9,... | collective-permute-start | bytes 12296 | tf_op jit(solution)/shard_map/ppermute | solution.py:19
  101.1 4.9 %collective-permute-start.1 = (f32[8,32,4]{2,1,0:T(8,128)S(1)}, f32[8,32,4]{2,1,0:T(8,128)S(1)}, u32[]{:S(2)}, u32[]{:S(2)}) collective-permute-start(f32[8,32,4]{2,1,0:T(8,128)S(1)} %get-tuple-element.49), channel_id=1, source_target_pairs={{4,0},{8,4},{12,8},{16,12},{20,16},{24,20},{28,24},{5,1},{9,5},{13... | collective-permute-start | bytes 12296 | tf_op jit(solution)/shard_map/ppermute | solution.py:20
  106.3 8.2 %collective-permute-start.2 = (f32[8,4,72]{1,2,0:T(8,128)S(1)}, f32[8,4,72]{1,2,0:T(8,128)S(1)}, u32[]{:S(2)}, u32[]{:S(2)}) collective-permute-start(f32[8,4,72]{1,2,0:T(8,128)S(1)} %copy.233), channel_id=1, source_target_pairs={{0,1},{1,2},{2,3},{4,5},{5,6},{6,7},{8,9},{9,10},{10,11},{12,13},{... | collective-permute-start | bytes 27656 | tf_op jit(solution)/shard_map/ppermute | solution.py:19
  109.8 10.3 %copy-start.6 = (f32[36,68]{0,1:T(8,128)S(1)}, f32[36,68]{0,1:T(8,128)}, u32[]{:S(2)}) copy-start(f32[36,68]{0,1:T(8,128)} %and_convert_fusion.1) | copy-start | bytes 29380
  109.9 9.5 %collective-permute-start.3 = (f32[8,4,72]{1,2,0:T(8,128)S(1)}, f32[8,4,72]{1,2,0:T(8,128)S(1)}, u32[]{:S(2)}, u32[]{:S(2)}) collective-permute-start(f32[8,4,72]{1,2,0:T(8,128)S(1)} %copy.234), channel_id=1, source_target_pairs={{1,0},{2,1},{3,2},{5,4},{6,5},{7,6},{9,8},{10,9},{11,10},{13,12},{... | collective-permute-start | bytes 27656 | tf_op jit(solution)/shard_map/ppermute | solution.py:20
  121.7 5.3 %collective-permute-start.8 = (f32[8,32,1]{1,2,0:T(1,128)S(1)}, f32[8,32,1]{1,2,0:T(1,128)S(1)}, u32[]{:S(2)}, u32[]{:S(2)}) collective-permute-start(f32[8,32,1]{1,2,0:T(1,128)S(1)} %get-tuple-element.40), channel_id=1, source_target_pairs={{0,4},{4,8},{8,12},{12,16},{16,20},{20,24},{24,28},{1,5},{5,9},{9,... | collective-permute-start | bytes 3080 | tf_op jit(solution)/shard_map/ppermute | solution.py:19
  125.8 4.8 %collective-permute-start.9 = (f32[8,32,1]{1,2,0:T(1,128)S(1)}, f32[8,32,1]{1,2,0:T(1,128)S(1)}, u32[]{:S(2)}, u32[]{:S(2)}) collective-permute-start(f32[8,32,1]{1,2,0:T(1,128)S(1)} %get-tuple-element.41), channel_id=1, source_target_pairs={{4,0},{8,4},{12,8},{16,12},{20,16},{24,20},{28,24},{5,1},{9,5},{13... | collective-permute-start | bytes 3080 | tf_op jit(solution)/shard_map/ppermute | solution.py:20
  130.8 10.4 %collective-permute-start.10 = (f32[8,1,66]{1,2,0:T(8,128)S(1)}, f32[8,1,66]{1,2,0:T(8,128)S(1)}, u32[]{:S(2)}, u32[]{:S(2)}) collective-permute-start(f32[8,1,66]{1,2,0:T(8,128)S(1)} %get-tuple-element.29), channel_id=1, source_target_pairs={{1,0},{2,1},{3,2},{5,4},{6,5},{7,6},{9,8},{10,9},{11,10},{13,12},{... | collective-permute-start | bytes 6344 | tf_op jit(solution)/shard_map/ppermute | solution.py:20
  132.1 10.8 %collective-permute-start.11 = (f32[8,1,66]{1,2,0:T(8,128)S(1)}, f32[8,1,66]{1,2,0:T(8,128)S(1)}, u32[]{:S(2)}, u32[]{:S(2)}) collective-permute-start(f32[8,1,66]{1,2,0:T(8,128)S(1)} %get-tuple-element.28), channel_id=1, source_target_pairs={{0,1},{1,2},{2,3},{4,5},{5,6},{6,7},{8,9},{9,10},{10,11},{12,13},{... | collective-permute-start | bytes 6344 | tf_op jit(solution)/shard_map/ppermute | solution.py:19
  143.7 4.5 %collective-permute-start.12 = (f32[8,32,1]{1,2,0:T(1,128)S(1)}, f32[8,32,1]{1,2,0:T(1,128)S(1)}, u32[]{:S(2)}, u32[]{:S(2)}) collective-permute-start(f32[8,32,1]{1,2,0:T(1,128)S(1)} %get-tuple-element.38), channel_id=1, source_target_pairs={{0,4},{4,8},{8,12},{12,16},{16,20},{20,24},{24,28},{1,5},{5,9},{9,... | collective-permute-start | bytes 3080 | tf_op jit(solution)/shard_map/ppermute | solution.py:19
  146.8 3.1 %collective-permute-start.13 = (f32[8,32,1]{1,2,0:T(1,128)S(1)}, f32[8,32,1]{1,2,0:T(1,128)S(1)}, u32[]{:S(2)}, u32[]{:S(2)}) collective-permute-start(f32[8,32,1]{1,2,0:T(1,128)S(1)} %get-tuple-element.39), channel_id=1, source_target_pairs={{4,0},{8,4},{12,8},{16,12},{20,16},{24,20},{28,24},{5,1},{9,5},{13... | collective-permute-start | bytes 3080 | tf_op jit(solution)/shard_map/ppermute | solution.py:20
  150.1 10.3 %collective-permute-start.14 = (f32[8,1,66]{1,2,0:T(8,128)S(1)}, f32[8,1,66]{1,2,0:T(8,128)S(1)}, u32[]{:S(2)}, u32[]{:S(2)}) collective-permute-start(f32[8,1,66]{1,2,0:T(8,128)S(1)} %get-tuple-element.27), channel_id=1, source_target_pairs={{1,0},{2,1},{3,2},{5,4},{6,5},{7,6},{9,8},{10,9},{11,10},{13,12},{... | collective-permute-start | bytes 6344 | tf_op jit(solution)/shard_map/ppermute | solution.py:20
  151.4 10.8 %collective-permute-start.15 = (f32[8,1,66]{1,2,0:T(8,128)S(1)}, f32[8,1,66]{1,2,0:T(8,128)S(1)}, u32[]{:S(2)}, u32[]{:S(2)}) collective-permute-start(f32[8,1,66]{1,2,0:T(8,128)S(1)} %get-tuple-element.26), channel_id=1, source_target_pairs={{0,1},{1,2},{2,3},{4,5},{5,6},{6,7},{8,9},{9,10},{10,11},{12,13},{... | collective-permute-start | bytes 6344 | tf_op jit(solution)/shard_map/ppermute | solution.py:19
  162.9 4.8 %collective-permute-start.16 = (f32[8,32,1]{1,2,0:T(1,128)S(1)}, f32[8,32,1]{1,2,0:T(1,128)S(1)}, u32[]{:S(2)}, u32[]{:S(2)}) collective-permute-start(f32[8,32,1]{1,2,0:T(1,128)S(1)} %get-tuple-element.36), channel_id=1, source_target_pairs={{0,4},{4,8},{8,12},{12,16},{16,20},{20,24},{24,28},{1,5},{5,9},{9,... | collective-permute-start | bytes 3080 | tf_op jit(solution)/shard_map/ppermute | solution.py:19
  166.5 3.1 %collective-permute-start.17 = (f32[8,32,1]{1,2,0:T(1,128)S(1)}, f32[8,32,1]{1,2,0:T(1,128)S(1)}, u32[]{:S(2)}, u32[]{:S(2)}) collective-permute-start(f32[8,32,1]{1,2,0:T(1,128)S(1)} %get-tuple-element.37), channel_id=1, source_target_pairs={{4,0},{8,4},{12,8},{16,12},{20,16},{24,20},{28,24},{5,1},{9,5},{13... | collective-permute-start | bytes 3080 | tf_op jit(solution)/shard_map/ppermute | solution.py:20
  169.7 10.4 %collective-permute-start.18 = (f32[8,1,66]{1,2,0:T(8,128)S(1)}, f32[8,1,66]{1,2,0:T(8,128)S(1)}, u32[]{:S(2)}, u32[]{:S(2)}) collective-permute-start(f32[8,1,66]{1,2,0:T(8,128)S(1)} %get-tuple-element.25), channel_id=1, source_target_pairs={{1,0},{2,1},{3,2},{5,4},{6,5},{7,6},{9,8},{10,9},{11,10},{13,12},{... | collective-permute-start | bytes 6344 | tf_op jit(solution)/shard_map/ppermute | solution.py:20
  171.0 10.9 %collective-permute-start.19 = (f32[8,1,66]{1,2,0:T(8,128)S(1)}, f32[8,1,66]{1,2,0:T(8,128)S(1)}, u32[]{:S(2)}, u32[]{:S(2)}) collective-permute-start(f32[8,1,66]{1,2,0:T(8,128)S(1)} %get-tuple-element.24), channel_id=1, source_target_pairs={{0,1},{1,2},{2,3},{4,5},{5,6},{6,7},{8,9},{9,10},{10,11},{12,13},{... | collective-permute-start | bytes 6344 | tf_op jit(solution)/shard_map/ppermute | solution.py:19
  182.7 4.8 %collective-permute-start.20 = (f32[8,32,1]{1,2,0:T(1,128)S(1)}, f32[8,32,1]{1,2,0:T(1,128)S(1)}, u32[]{:S(2)}, u32[]{:S(2)}) collective-permute-start(f32[8,32,1]{1,2,0:T(1,128)S(1)} %get-tuple-element.30), channel_id=1, source_target_pairs={{0,4},{4,8},{8,12},{12,16},{16,20},{20,24},{24,28},{1,5},{5,9},{9,... | collective-permute-start | bytes 3080 | tf_op jit(solution)/shard_map/ppermute | solution.py:19
  186.2 3.3 %collective-permute-start.21 = (f32[8,32,1]{1,2,0:T(1,128)S(1)}, f32[8,32,1]{1,2,0:T(1,128)S(1)}, u32[]{:S(2)}, u32[]{:S(2)}) collective-permute-start(f32[8,32,1]{1,2,0:T(1,128)S(1)} %get-tuple-element.31), channel_id=1, source_target_pairs={{4,0},{8,4},{12,8},{16,12},{20,16},{24,20},{28,24},{5,1},{9,5},{13... | collective-permute-start | bytes 3080 | tf_op jit(solution)/shard_map/ppermute | solution.py:20
  189.6 10.6 %collective-permute-start.22 = (f32[8,1,66]{1,2,0:T(8,128)S(1)}, f32[8,1,66]{1,2,0:T(8,128)S(1)}, u32[]{:S(2)}, u32[]{:S(2)}) collective-permute-start(f32[8,1,66]{1,2,0:T(8,128)S(1)} %get-tuple-element.23), channel_id=1, source_target_pairs={{1,0},{2,1},{3,2},{5,4},{6,5},{7,6},{9,8},{10,9},{11,10},{13,12},{... | collective-permute-start | bytes 6344 | tf_op jit(solution)/shard_map/ppermute | solution.py:20
  190.9 11.0 %collective-permute-start.23 = (f32[8,1,66]{1,2,0:T(8,128)S(1)}, f32[8,1,66]{1,2,0:T(8,128)S(1)}, u32[]{:S(2)}, u32[]{:S(2)}) collective-permute-start(f32[8,1,66]{1,2,0:T(8,128)S(1)} %get-tuple-element.22), channel_id=1, source_target_pairs={{0,1},{1,2},{2,3},{4,5},{5,6},{6,7},{8,9},{9,10},{10,11},{12,13},{... | collective-permute-start | bytes 6344 | tf_op jit(solution)/shard_map/ppermute | solution.py:19
  221.5 28.3 %copy-start.4 = (bf16[8,4,8,128]{3,2,1,0:T(8,128)(2,1)S(1)}, bf16[8,4,8,128]{3,2,1,0:T(8,128)(2,1)}, u32[]{:S(2)}) copy-start(bf16[8,4,8,128]{3,2,1,0:T(8,128)(2,1)} %param.8) | copy-start | bytes 196612
  (8 other events, 15.1 us)
Sparse Core Ops, SparseCore 0:
  10.1 48.3 all-gather.1
  65.6 32.8 reduce-scatter.6
  225.1 24.6 reduce-scatter.4
where the time goes:
time: 259 us; the launch traced here: 258 us
  waiting for transfers between devices  136 us (53%)
  starting transfers between devices  58.4 us (23%)
  blocking collectives  17.4 us (7%)
  between operations  14.5 us (6%)
  local copies, waits for them, and re-layouts  11.8 us (5%)
  other arithmetic  10.6 us (4%)
  matrix products  9.04 us (3%)
    ppermute x12, starting transfers between devices, padded_2(): before = lax.ppermute(last, axis, up)  42.8 us
    all_gather x1, waiting for transfers between devices, body(): lax.all_gather(widened, 'lat', axis=0, tiled=True)  39.5 us
    ppermute x12, waiting for transfers between devices, padded_2(): after = lax.ppermute(initial, axis, down)  38.1 us
    reduce_scatter x1, waiting for transfers between devices, body(): lax.psum_scatter(jnp.einsum('rc,mlrw->cmlw', columns, projected, precisio...  24.8 us
    unnamed x4, waiting for transfers between devices  24.4 us
    all_gather x1, blocking collectives, body(): lax.all_gather(adjoint, 'mem', axis=2, tiled=True)[None]  17.4 us
    ppermute x12, starting transfers between devices, padded_2(): after = lax.ppermute(initial, axis, down)  15.5 us
    ppermute x12, waiting for transfers between devices, padded_2(): before = lax.ppermute(last, axis, up)  9.46 us
  transfers between devices with their start and end apart: 27, of which 19 were waited for; matrix products, arithmetic and copies ran while one was open for 6% of the time, Pallas kernels for 0%

commit v1 on v0

--- a/solution.py
+++ b/solution.py
@@ -7,6 +7,11 @@
 OBLK = 8
 diffusion = 0.2
 highest = lax.Precision.HIGHEST
+
+
+def tiled_gather(x, axis, dim):
+    copies = jnp.concatenate([x] * lax.axis_size(axis), axis=dim)
+    return lax.all_to_all(copies, axis, dim, dim, tiled=True)
 
 
 def padded_2(value, sides, width):
@@ -95,10 +100,7 @@
     )
     columns = lat_full
     localized = jnp.einsum(
-        "rc,cmlf->mlrf",
-        columns,
-        lax.all_gather(widened, "lat", axis=0, tiled=True),
-        precision=highest,
+        "rc,cmlf->mlrf", columns, tiled_gather(widened, "lat", 0), precision=highest
     )
     partial_sum = jnp.sum(localized * perturbations, axis=0)
     increment = lax.psum_scatter(partial_sum, "mem", scatter_dimension=2, tiled=True) * member_scale

time: 259 us -> 267 us (1.031)
  starting transfers between devices: 58.4 us -> 63.2 us
  waiting for transfers between devices: 136 us -> 140 us
    all_to_all x0 -> x1, waiting for transfers between devices: none -> 41.7 us  [tiled_gather(): return lax.all_to_all(copies, axis, dim, dim, tiled=True)]
    all_gather x1 -> x0, waiting for transfers between devices: 39.5 us -> none  [body(): lax.all_gather(widened, 'lat', axis=0, tiled=True)]
    all_to_all x0 -> x1, starting transfers between devices: none -> 6.48 us  [tiled_gather(): return lax.all_to_all(copies, axis, dim, dim, tiled=True)]
    unnamed x4 -> x3, waiting for transfers between devices: 24.4 us -> 26.3 us
    unnamed x31 -> x27, local copies, waits for them, and re-layouts: 5.89 us -> 5.93 us
  transfers between devices with their start and end apart: 27 -> 27, of which waited for: 19 -> 19; matrix products, arithmetic and copies ran while one was open for 6% -> 5% of each run, Pallas kernels for 0% -> 0%
where the time goes in v1:
time: 267 us; the launch traced here: 266 us
  waiting for transfers between devices  140 us (52%)
  starting transfers between devices  63.2 us (24%)
  blocking collectives  17.2 us (6%)
  between operations  14.7 us (6%)
  local copies, waits for them, and re-layouts  13.6 us (5%)
  other arithmetic  9.33 us (3%)
  matrix products  7.93 us (3%)
    all_to_all x1, waiting for transfers between devices, tiled_gather(): return lax.all_to_all(copies, axis, dim, dim, tiled=True)  41.7 us
    ppermute x12, starting transfers between devices, padded_2(): before = lax.ppermute(last, axis, up)  41.2 us
    ppermute x12, waiting for transfers between devices, padded_2(): after = lax.ppermute(initial, axis, down)  37.9 us
    unnamed x3, waiting for transfers between devices  26.3 us
    reduce_scatter x1, waiting for transfers between devices, body(): lax.psum_scatter(jnp.einsum('rc,mlrw->cmlw', columns, projected, precisio...  24.7 us
    all_gather x1, blocking collectives, body(): lax.all_gather(adjoint, 'mem', axis=2, tiled=True)[None]  17.2 us
    ppermute x12, starting transfers between devices, padded_2(): after = lax.ppermute(initial, axis, down)  15.5 us
    ppermute x12, waiting for transfers between devices, padded_2(): before = lax.ppermute(last, axis, up)  9.46 us
  transfers between devices with their start and end apart: 27, of which 19 were waited for; matrix products, arithmetic and copies ran while one was open for 5% of the time, Pallas kernels for 0%

profile of v1, /device:TPU:0, one launch (start us, length us, event | category | flops | bytes accessed | tf_op | source)
XLA Modules:
  0.0 266.2 jit_solution(16705029233673162082)
XLA Ops:
  9.4 2.6 copy.237
  12.0 6.5 %all-to-all-start = ((f32[32,4,8,512]{3,2,1,0:T(8,128)}), f32[32,4,8,512]{3,2,1,0:T(8,128)S(1)}, u32[]{:S(2)}, u32[]{:S(2)}) async-start(f32[32,4,8,512]{3,2,1,0:T(8,128)} %copy.237), calls=%async_computation | async-start | bytes 4194304 | tf_op jit(solution)/shard_map/all_to_all | solution.py:14
  24.9 41.7 %all-to-all-done = f32[32,4,8,512]{3,2,1,0:T(8,128)S(1)} async-done(((f32[32,4,8,512]{3,2,1,0:T(8,128)}), f32[32,4,8,512]{3,2,1,0:T(8,128)S(1)}, u32[]{:S(2)}, u32[]{:S(2)}) %all-to-all-start) | async-done | bytes 2097184 | tf_op jit(solution)/shard_map/all_to_all | solution.py:14
  66.6 3.4 %fusion = f32[8,32,512]{2,1,0:T(8,128)} fusion(bf16[4,8,32,512]{3,2,1,0:T(8,128)(2,1)S(1)} %copy-done.1, f32[32,4,8,512]{3,2,1,0:T(8,128)S(1)} %all-to-all-done, bf16[32,32]{1,0:T(8,128)(2,1)S(1)} %copy-done.10), kind=kOutput, calls=%fused_computation.2 | convolution fusion | flops 202768384 | bytes 3672064 | tf_op jit(solution)/shard_map/rc,cmlf->mlrf/dot_general | solution.py:102
  70.1 1.8 copy.260
  76.4 3.9 %collective-permute-done.7 = f32[2,4,72]{2,1,0:T(4,128)S(1)} collective-permute-done((f32[2,4,72]{2,1,0:T(4,128)S(1)}, f32[2,4,72]{2,1,0:T(4,128)S(1)}, u32[]{:S(2)}, u32[]{:S(2)}) %collective-permute-start.7) | collective-permute-done | bytes 2336 | tf_op jit(solution)/shard_map/ppermute | solution.py:25
  80.4 26.3 %reduce-scatter.7.cloned.1.call-done = f32[64,256]{1,0:T(8,128)} async-done(((f32[512,256]{1,0:T(8,128)}), f32[64,256]{1,0:T(8,128)}) %reduce-scatter.7.cloned.1.call-update) | async-done | bytes 65552
  110.6 3.5 %collective-permute-done.1 = f32[8,32,4]{2,1,0:T(8,128)S(1)} collective-permute-done((f32[8,32,4]{2,1,0:T(8,128)S(1)}, f32[8,32,4]{2,1,0:T(8,128)S(1)}, u32[]{:S(2)}, u32[]{:S(2)}) %collective-permute-start.1) | collective-permute-done | bytes 4128 | tf_op jit(solution)/shard_map/ppermute | solution.py:25
  114.5 3.4 %collective-permute-start.2 = (f32[8,4,72]{1,2,0:T(8,128)S(1)}, f32[8,4,72]{1,2,0:T(8,128)S(1)}, u32[]{:S(2)}, u32[]{:S(2)}) collective-permute-start(f32[8,4,72]{1,2,0:T(8,128)S(1)} %copy.239), channel_id=1, source_target_pairs={{0,1},{1,2},{2,3},{4,5},{5,6},{6,7},{8,9},{9,10},{10,11},{12,13},{... | collective-permute-start | bytes 27656 | tf_op jit(solution)/shard_map/ppermute | solution.py:24
  120.2 2.5 collective-permute-done.2
  122.7 4.9 %collective-permute-done.3 = f32[8,4,72]{1,2,0:T(8,128)S(1)} collective-permute-done((f32[8,4,72]{1,2,0:T(8,128)S(1)}, f32[8,4,72]{1,2,0:T(8,128)S(1)}, u32[]{:S(2)}, u32[]{:S(2)}) %collective-permute-start.3) | collective-permute-done | bytes 9248 | tf_op jit(solution)/shard_map/ppermute | solution.py:25
  129.9 4.0 %collective-permute-start.8 = (f32[8,32,1]{1,2,0:T(1,128)S(1)}, f32[8,32,1]{1,2,0:T(1,128)S(1)}, u32[]{:S(2)}, u32[]{:S(2)}) collective-permute-start(f32[8,32,1]{1,2,0:T(1,128)S(1)} %get-tuple-element.40), channel_id=1, source_target_pairs={{0,4},{4,8},{8,12},{12,16},{16,20},{20,24},{24,28},{1,5},{5,9},{9,... | collective-permute-start | bytes 3080 | tf_op jit(solution)/shard_map/ppermute | solution.py:24
  135.2 3.5 %collective-permute-done.9 = f32[8,32,1]{1,2,0:T(1,128)S(1)} collective-permute-done((f32[8,32,1]{1,2,0:T(1,128)S(1)}, f32[8,32,1]{1,2,0:T(1,128)S(1)}, u32[]{:S(2)}, u32[]{:S(2)}) %collective-permute-start.9) | collective-permute-done | bytes 1056 | tf_op jit(solution)/shard_map/ppermute | solution.py:25
  140.2 4.6 %collective-permute-start.11 = (f32[8,1,66]{1,2,0:T(8,128)S(1)}, f32[8,1,66]{1,2,0:T(8,128)S(1)}, u32[]{:S(2)}, u32[]{:S(2)}) collective-permute-start(f32[8,1,66]{1,2,0:T(8,128)S(1)} %get-tuple-element.28), channel_id=1, source_target_pairs={{0,1},{1,2},{2,3},{4,5},{5,6},{6,7},{8,9},{9,10},{10,11},{12,13},{... | collective-permute-start | bytes 6344 | tf_op jit(solution)/shard_map/ppermute | solution.py:24
  145.0 4.3 %collective-permute-done.10 = f32[8,1,66]{1,2,0:T(8,128)S(1)} collective-permute-done((f32[8,1,66]{1,2,0:T(8,128)S(1)}, f32[8,1,66]{1,2,0:T(8,128)S(1)}, u32[]{:S(2)}, u32[]{:S(2)}) %collective-permute-start.10) | collective-permute-done | bytes 2144 | tf_op jit(solution)/shard_map/ppermute | solution.py:25
  149.3 1.7 collective-permute-done.11
  151.9 3.1 %collective-permute-start.12 = (f32[8,32,1]{1,2,0:T(1,128)S(1)}, f32[8,32,1]{1,2,0:T(1,128)S(1)}, u32[]{:S(2)}, u32[]{:S(2)}) collective-permute-start(f32[8,32,1]{1,2,0:T(1,128)S(1)} %get-tuple-element.38), channel_id=1, source_target_pairs={{0,4},{4,8},{8,12},{12,16},{16,20},{20,24},{24,28},{1,5},{5,9},{9,... | collective-permute-start | bytes 3080 | tf_op jit(solution)/shard_map/ppermute | solution.py:24
  156.3 1.8 collective-permute-done.13
  159.6 5.0 %collective-permute-start.15 = (f32[8,1,66]{1,2,0:T(8,128)S(1)}, f32[8,1,66]{1,2,0:T(8,128)S(1)}, u32[]{:S(2)}, u32[]{:S(2)}) collective-permute-start(f32[8,1,66]{1,2,0:T(8,128)S(1)} %get-tuple-element.26), channel_id=1, source_target_pairs={{0,1},{1,2},{2,3},{4,5},{5,6},{6,7},{8,9},{9,10},{10,11},{12,13},{... | collective-permute-start | bytes 6344 | tf_op jit(solution)/shard_map/ppermute | solution.py:24
  164.6 3.9 %collective-permute-done.14 = f32[8,1,66]{1,2,0:T(8,128)S(1)} collective-permute-done((f32[8,1,66]{1,2,0:T(8,128)S(1)}, f32[8,1,66]{1,2,0:T(8,128)S(1)}, u32[]{:S(2)}, u32[]{:S(2)}) %collective-permute-start.14) | collective-permute-done | bytes 2144 | tf_op jit(solution)/shard_map/ppermute | solution.py:25
  168.6 1.7 collective-permute-done.15
  171.1 3.5 %collective-permute-start.16 = (f32[8,32,1]{1,2,0:T(1,128)S(1)}, f32[8,32,1]{1,2,0:T(1,128)S(1)}, u32[]{:S(2)}, u32[]{:S(2)}) collective-permute-start(f32[8,32,1]{1,2,0:T(1,128)S(1)} %get-tuple-element.36), channel_id=1, source_target_pairs={{0,4},{4,8},{8,12},{12,16},{16,20},{20,24},{24,28},{1,5},{5,9},{9,... | collective-permute-start | bytes 3080 | tf_op jit(solution)/shard_map/ppermute | solution.py:24
  175.9 1.8 collective-permute-done.17
  179.2 5.0 %collective-permute-start.19 = (f32[8,1,66]{1,2,0:T(8,128)S(1)}, f32[8,1,66]{1,2,0:T(8,128)S(1)}, u32[]{:S(2)}, u32[]{:S(2)}) collective-permute-start(f32[8,1,66]{1,2,0:T(8,128)S(1)} %get-tuple-element.24), channel_id=1, source_target_pairs={{0,1},{1,2},{2,3},{4,5},{5,6},{6,7},{8,9},{9,10},{10,11},{12,13},{... | collective-permute-start | bytes 6344 | tf_op jit(solution)/shard_map/ppermute | solution.py:24
  184.1 4.2 %collective-permute-done.18 = f32[8,1,66]{1,2,0:T(8,128)S(1)} collective-permute-done((f32[8,1,66]{1,2,0:T(8,128)S(1)}, f32[8,1,66]{1,2,0:T(8,128)S(1)}, u32[]{:S(2)}, u32[]{:S(2)}) %collective-permute-start.18) | collective-permute-done | bytes 2144 | tf_op jit(solution)/shard_map/ppermute | solution.py:25
  190.8 3.5 %collective-permute-start.20 = (f32[8,32,1]{1,2,0:T(1,128)S(1)}, f32[8,32,1]{1,2,0:T(1,128)S(1)}, u32[]{:S(2)}, u32[]{:S(2)}) collective-permute-start(f32[8,32,1]{1,2,0:T(1,128)S(1)} %get-tuple-element.30), channel_id=1, source_target_pairs={{0,4},{4,8},{8,12},{12,16},{16,20},{20,24},{24,28},{1,5},{5,9},{9,... | collective-permute-start | bytes 3080 | tf_op jit(solution)/shard_map/ppermute | solution.py:24
  195.6 2.0 collective-permute-done.21
  199.1 5.0 %collective-permute-start.23 = (f32[8,1,66]{1,2,0:T(8,128)S(1)}, f32[8,1,66]{1,2,0:T(8,128)S(1)}, u32[]{:S(2)}, u32[]{:S(2)}) collective-permute-start(f32[8,1,66]{1,2,0:T(8,128)S(1)} %get-tuple-element.22), channel_id=1, source_target_pairs={{0,1},{1,2},{2,3},{4,5},{5,6},{6,7},{8,9},{9,10},{10,11},{12,13},{... | collective-permute-start | bytes 6344 | tf_op jit(solution)/shard_map/ppermute | solution.py:24
  204.1 4.2 %collective-permute-done.22 = f32[8,1,66]{1,2,0:T(8,128)S(1)} collective-permute-done((f32[8,1,66]{1,2,0:T(8,128)S(1)}, f32[8,1,66]{1,2,0:T(8,128)S(1)}, u32[]{:S(2)}, u32[]{:S(2)}) %collective-permute-start.22) | collective-permute-done | bytes 2144 | tf_op jit(solution)/shard_map/ppermute | solution.py:25
  210.8 17.2 %all_gather.3 = f32[8,32,512]{1,2,0:T(8,128)S(1)} all-gather(f32[8,32,64]{1,2,0:T(8,128)S(1)} %fusion.8), channel_id=1, replica_groups=mesh['mem'=8,'lat'=4] {'mem'}, dimensions={2}, use_global_device_ids=true | all-gather | bytes 589824 | tf_op jit(solution)/shard_map/all_gather | solution.py:134
  229.5 2.2 fusion.1
  232.9 24.7 %reduce-scatter.5.cloned.1.call-done = f32[8,4,8,128]{3,0,2,1:T(8,128)} async-done(((f32[32,4,8,128]{3,0,2,1:T(8,128)}), f32[8,4,8,128]{3,0,2,1:T(8,128)}) %reduce-scatter.5.cloned.1.call-update) | async-done | bytes 131088 | tf_op jit(solution)/shard_map/reduce_scatter | solution.py:137
  (127 shorter events, 43.9 us)
Async XLA Ops:
  12.0 54.7 %copy-start.1 = (bf16[4,8,32,512]{3,2,1,0:T(8,128)(2,1)S(1)}, bf16[4,8,32,512]{3,2,1,0:T(8,128)(2,1)}, u32[]{:S(2)}) copy-start(bf16[4,8,32,512]{3,2,1,0:T(8,128)(2,1)} %param.9) | copy-start | bytes 3145732
  12.0 54.7 %copy-start.10 = (bf16[32,32]{1,0:T(8,128)(2,1)S(1)}, bf16[32,32]{1,0:T(8,128)(2,1)}, u32[]{:S(2)}) copy-start(bf16[32,32]{1,0:T(8,128)(2,1)} %param.10) | copy-start | bytes 6148
  12.0 54.7 %all-to-all-start = ((f32[32,4,8,512]{3,2,1,0:T(8,128)}), f32[32,4,8,512]{3,2,1,0:T(8,128)S(1)}, u32[]{:S(2)}, u32[]{:S(2)}) async-start(f32[32,4,8,512]{3,2,1,0:T(8,128)} %copy.237), calls=%async_computation | async-start | bytes 4194304 | tf_op jit(solution)/shard_map/all_to_all | solution.py:14
  18.4 88.3 %reduce-scatter.7.cloned.1.call-start = ((), (), s32[]{:S(2)}) async-start(), calls=%async_computation.4 | async-start | bytes 589824
  19.1 54.2 %collective-permute-start.4 = (f32[2,32,4]{2,1,0:T(8,128)}, f32[2,32,4]{2,1,0:T(8,128)S(1)}, u32[]{:S(2)}, u32[]{:S(2)}) collective-permute-start(f32[2,32,4]{2,1,0:T(8,128)} %get-tuple-element.62), channel_id=1, source_target_pairs={{0,4},{4,8},{8,12},{12,16},{16,20},{20,24},{24,28},{1,5},{5,9},{9,... | collective-permute-start | bytes 3080 | tf_op jit(solution)/shard_map/ppermute | solution.py:24
  20.6 52.8 %collective-permute-start.5 = (f32[2,32,4]{2,1,0:T(8,128)}, f32[2,32,4]{2,1,0:T(8,128)S(1)}, u32[]{:S(2)}, u32[]{:S(2)}) collective-permute-start(f32[2,32,4]{2,1,0:T(8,128)} %get-tuple-element.63), channel_id=1, source_target_pairs={{4,0},{8,4},{12,8},{16,12},{20,16},{24,20},{28,24},{5,1},{9,5},{13... | collective-permute-start | bytes 3080 | tf_op jit(solution)/shard_map/ppermute | solution.py:25
  73.3 184.4 %reduce-scatter.5.cloned.1.call-start = ((), (), s32[]{:S(2)}) async-start(), calls=%async_computation.3 | async-start | bytes 655360 | tf_op jit(solution)/shard_map/reduce_scatter | solution.py:137
  73.5 2.9 %collective-permute-start.6 = (f32[2,4,72]{2,1,0:T(4,128)S(1)}, f32[2,4,72]{2,1,0:T(4,128)S(1)}, u32[]{:S(2)}, u32[]{:S(2)}) collective-permute-start(f32[2,4,72]{2,1,0:T(4,128)S(1)} %get-tuple-element.50), channel_id=1, source_target_pairs={{0,1},{1,2},{2,3},{4,5},{5,6},{6,7},{8,9},{9,10},{10,11},{12,13},{... | collective-permute-start | bytes 6920 | tf_op jit(solution)/shard_map/ppermute | solution.py:24
  74.8 5.5 %collective-permute-start.7 = (f32[2,4,72]{2,1,0:T(4,128)S(1)}, f32[2,4,72]{2,1,0:T(4,128)S(1)}, u32[]{:S(2)}, u32[]{:S(2)}) collective-permute-start(f32[2,4,72]{2,1,0:T(4,128)S(1)} %get-tuple-element.51), channel_id=1, source_target_pairs={{1,0},{2,1},{3,2},{5,4},{6,5},{7,6},{9,8},{10,9},{11,10},{13,12},{... | collective-permute-start | bytes 6920 | tf_op jit(solution)/shard_map/ppermute | solution.py:25
  107.8 20.0 %copy-start.7 = (f32[38,70]{0,1:T(8,128)S(1)}, f32[38,70]{0,1:T(8,128)}, u32[]{:S(2)}) copy-start(f32[38,70]{0,1:T(8,128)} %and_convert_fusion.2) | copy-start | bytes 31924
  107.8 20.4 %copy-start.2 = (f32[8,32,64]{2,1,0:T(8,128)}, f32[8,32,64]{2,1,0:T(8,128)S(1)}, u32[]{:S(2)}) copy-start(f32[8,32,64]{2,1,0:T(8,128)S(1)} %broadcast_multiply_fusion.8) | copy-start | bytes 196612
  107.9 2.7 %collective-permute-start = (f32[8,32,4]{2,1,0:T(8,128)S(1)}, f32[8,32,4]{2,1,0:T(8,128)S(1)}, u32[]{:S(2)}, u32[]{:S(2)}) collective-permute-start(f32[8,32,4]{2,1,0:T(8,128)S(1)} %get-tuple-element.48), channel_id=1, source_target_pairs={{0,4},{4,8},{8,12},{12,16},{16,20},{20,24},{24,28},{1,5},{5,9},{9,... | collective-permute-start | bytes 12296 | tf_op jit(solution)/shard_map/ppermute | solution.py:24
  109.2 4.9 %collective-permute-start.1 = (f32[8,32,4]{2,1,0:T(8,128)S(1)}, f32[8,32,4]{2,1,0:T(8,128)S(1)}, u32[]{:S(2)}, u32[]{:S(2)}) collective-permute-start(f32[8,32,4]{2,1,0:T(8,128)S(1)} %get-tuple-element.49), channel_id=1, source_target_pairs={{4,0},{8,4},{12,8},{16,12},{20,16},{24,20},{28,24},{5,1},{9,5},{13... | collective-permute-start | bytes 12296 | tf_op jit(solution)/shard_map/ppermute | solution.py:25
  114.5 8.2 %collective-permute-start.2 = (f32[8,4,72]{1,2,0:T(8,128)S(1)}, f32[8,4,72]{1,2,0:T(8,128)S(1)}, u32[]{:S(2)}, u32[]{:S(2)}) collective-permute-start(f32[8,4,72]{1,2,0:T(8,128)S(1)} %copy.239), channel_id=1, source_target_pairs={{0,1},{1,2},{2,3},{4,5},{5,6},{6,7},{8,9},{9,10},{10,11},{12,13},{... | collective-permute-start | bytes 27656 | tf_op jit(solution)/shard_map/ppermute | solution.py:24
  118.1 9.5 %collective-permute-start.3 = (f32[8,4,72]{1,2,0:T(8,128)S(1)}, f32[8,4,72]{1,2,0:T(8,128)S(1)}, u32[]{:S(2)}, u32[]{:S(2)}) collective-permute-start(f32[8,4,72]{1,2,0:T(8,128)S(1)} %copy.240), channel_id=1, source_target_pairs={{1,0},{2,1},{3,2},{5,4},{6,5},{7,6},{9,8},{10,9},{11,10},{13,12},{... | collective-permute-start | bytes 27656 | tf_op jit(solution)/shard_map/ppermute | solution.py:25
  129.9 5.3 %collective-permute-start.8 = (f32[8,32,1]{1,2,0:T(1,128)S(1)}, f32[8,32,1]{1,2,0:T(1,128)S(1)}, u32[]{:S(2)}, u32[]{:S(2)}) collective-permute-start(f32[8,32,1]{1,2,0:T(1,128)S(1)} %get-tuple-element.40), channel_id=1, source_target_pairs={{0,4},{4,8},{8,12},{12,16},{16,20},{20,24},{24,28},{1,5},{5,9},{9,... | collective-permute-start | bytes 3080 | tf_op jit(solution)/shard_map/ppermute | solution.py:24
  133.9 4.8 %collective-permute-start.9 = (f32[8,32,1]{1,2,0:T(1,128)S(1)}, f32[8,32,1]{1,2,0:T(1,128)S(1)}, u32[]{:S(2)}, u32[]{:S(2)}) collective-permute-start(f32[8,32,1]{1,2,0:T(1,128)S(1)} %get-tuple-element.41), channel_id=1, source_target_pairs={{4,0},{8,4},{12,8},{16,12},{20,16},{24,20},{28,24},{5,1},{9,5},{13... | collective-permute-start | bytes 3080 | tf_op jit(solution)/shard_map/ppermute | solution.py:25
  138.9 10.4 %collective-permute-start.10 = (f32[8,1,66]{1,2,0:T(8,128)S(1)}, f32[8,1,66]{1,2,0:T(8,128)S(1)}, u32[]{:S(2)}, u32[]{:S(2)}) collective-permute-start(f32[8,1,66]{1,2,0:T(8,128)S(1)} %get-tuple-element.29), channel_id=1, source_target_pairs={{1,0},{2,1},{3,2},{5,4},{6,5},{7,6},{9,8},{10,9},{11,10},{13,12},{... | collective-permute-start | bytes 6344 | tf_op jit(solution)/shard_map/ppermute | solution.py:25
  140.2 10.8 %collective-permute-start.11 = (f32[8,1,66]{1,2,0:T(8,128)S(1)}, f32[8,1,66]{1,2,0:T(8,128)S(1)}, u32[]{:S(2)}, u32[]{:S(2)}) collective-permute-start(f32[8,1,66]{1,2,0:T(8,128)S(1)} %get-tuple-element.28), channel_id=1, source_target_pairs={{0,1},{1,2},{2,3},{4,5},{5,6},{6,7},{8,9},{9,10},{10,11},{12,13},{... | collective-permute-start | bytes 6344 | tf_op jit(solution)/shard_map/ppermute | solution.py:24
  151.9 4.5 %collective-permute-start.12 = (f32[8,32,1]{1,2,0:T(1,128)S(1)}, f32[8,32,1]{1,2,0:T(1,128)S(1)}, u32[]{:S(2)}, u32[]{:S(2)}) collective-permute-start(f32[8,32,1]{1,2,0:T(1,128)S(1)} %get-tuple-element.38), channel_id=1, source_target_pairs={{0,4},{4,8},{8,12},{12,16},{16,20},{20,24},{24,28},{1,5},{5,9},{9,... | collective-permute-start | bytes 3080 | tf_op jit(solution)/shard_map/ppermute | solution.py:24
  155.0 3.1 %collective-permute-start.13 = (f32[8,32,1]{1,2,0:T(1,128)S(1)}, f32[8,32,1]{1,2,0:T(1,128)S(1)}, u32[]{:S(2)}, u32[]{:S(2)}) collective-permute-start(f32[8,32,1]{1,2,0:T(1,128)S(1)} %get-tuple-element.39), channel_id=1, source_target_pairs={{4,0},{8,4},{12,8},{16,12},{20,16},{24,20},{28,24},{5,1},{9,5},{13... | collective-permute-start | bytes 3080 | tf_op jit(solution)/shard_map/ppermute | solution.py:25
  158.3 10.3 %collective-permute-start.14 = (f32[8,1,66]{1,2,0:T(8,128)S(1)}, f32[8,1,66]{1,2,0:T(8,128)S(1)}, u32[]{:S(2)}, u32[]{:S(2)}) collective-permute-start(f32[8,1,66]{1,2,0:T(8,128)S(1)} %get-tuple-element.27), channel_id=1, source_target_pairs={{1,0},{2,1},{3,2},{5,4},{6,5},{7,6},{9,8},{10,9},{11,10},{13,12},{... | collective-permute-start | bytes 6344 | tf_op jit(solution)/shard_map/ppermute | solution.py:25
  159.6 10.7 %collective-permute-start.15 = (f32[8,1,66]{1,2,0:T(8,128)S(1)}, f32[8,1,66]{1,2,0:T(8,128)S(1)}, u32[]{:S(2)}, u32[]{:S(2)}) collective-permute-start(f32[8,1,66]{1,2,0:T(8,128)S(1)} %get-tuple-element.26), channel_id=1, source_target_pairs={{0,1},{1,2},{2,3},{4,5},{5,6},{6,7},{8,9},{9,10},{10,11},{12,13},{... | collective-permute-start | bytes 6344 | tf_op jit(solution)/shard_map/ppermute | solution.py:24
  171.1 4.8 %collective-permute-start.16 = (f32[8,32,1]{1,2,0:T(1,128)S(1)}, f32[8,32,1]{1,2,0:T(1,128)S(1)}, u32[]{:S(2)}, u32[]{:S(2)}) collective-permute-start(f32[8,32,1]{1,2,0:T(1,128)S(1)} %get-tuple-element.36), channel_id=1, source_target_pairs={{0,4},{4,8},{8,12},{12,16},{16,20},{20,24},{24,28},{1,5},{5,9},{9,... | collective-permute-start | bytes 3080 | tf_op jit(solution)/shard_map/ppermute | solution.py:24
  174.6 3.1 %collective-permute-start.17 = (f32[8,32,1]{1,2,0:T(1,128)S(1)}, f32[8,32,1]{1,2,0:T(1,128)S(1)}, u32[]{:S(2)}, u32[]{:S(2)}) collective-permute-start(f32[8,32,1]{1,2,0:T(1,128)S(1)} %get-tuple-element.37), channel_id=1, source_target_pairs={{4,0},{8,4},{12,8},{16,12},{20,16},{24,20},{28,24},{5,1},{9,5},{13... | collective-permute-start | bytes 3080 | tf_op jit(solution)/shard_map/ppermute | solution.py:25
  177.9 10.4 %collective-permute-start.18 = (f32[8,1,66]{1,2,0:T(8,128)S(1)}, f32[8,1,66]{1,2,0:T(8,128)S(1)}, u32[]{:S(2)}, u32[]{:S(2)}) collective-permute-start(f32[8,1,66]{1,2,0:T(8,128)S(1)} %get-tuple-element.25), channel_id=1, source_target_pairs={{1,0},{2,1},{3,2},{5,4},{6,5},{7,6},{9,8},{10,9},{11,10},{13,12},{... | collective-permute-start | bytes 6344 | tf_op jit(solution)/shard_map/ppermute | solution.py:25
  179.2 10.9 %collective-permute-start.19 = (f32[8,1,66]{1,2,0:T(8,128)S(1)}, f32[8,1,66]{1,2,0:T(8,128)S(1)}, u32[]{:S(2)}, u32[]{:S(2)}) collective-permute-start(f32[8,1,66]{1,2,0:T(8,128)S(1)} %get-tuple-element.24), channel_id=1, source_target_pairs={{0,1},{1,2},{2,3},{4,5},{5,6},{6,7},{8,9},{9,10},{10,11},{12,13},{... | collective-permute-start | bytes 6344 | tf_op jit(solution)/shard_map/ppermute | solution.py:24
  190.8 4.8 %collective-permute-start.20 = (f32[8,32,1]{1,2,0:T(1,128)S(1)}, f32[8,32,1]{1,2,0:T(1,128)S(1)}, u32[]{:S(2)}, u32[]{:S(2)}) collective-permute-start(f32[8,32,1]{1,2,0:T(1,128)S(1)} %get-tuple-element.30), channel_id=1, source_target_pairs={{0,4},{4,8},{8,12},{12,16},{16,20},{20,24},{24,28},{1,5},{5,9},{9,... | collective-permute-start | bytes 3080 | tf_op jit(solution)/shard_map/ppermute | solution.py:24
  194.3 3.3 %collective-permute-start.21 = (f32[8,32,1]{1,2,0:T(1,128)S(1)}, f32[8,32,1]{1,2,0:T(1,128)S(1)}, u32[]{:S(2)}, u32[]{:S(2)}) collective-permute-start(f32[8,32,1]{1,2,0:T(1,128)S(1)} %get-tuple-element.31), channel_id=1, source_target_pairs={{4,0},{8,4},{12,8},{16,12},{20,16},{24,20},{28,24},{5,1},{9,5},{13... | collective-permute-start | bytes 3080 | tf_op jit(solution)/shard_map/ppermute | solution.py:25
  197.8 10.6 %collective-permute-start.22 = (f32[8,1,66]{1,2,0:T(8,128)S(1)}, f32[8,1,66]{1,2,0:T(8,128)S(1)}, u32[]{:S(2)}, u32[]{:S(2)}) collective-permute-start(f32[8,1,66]{1,2,0:T(8,128)S(1)} %get-tuple-element.23), channel_id=1, source_target_pairs={{1,0},{2,1},{3,2},{5,4},{6,5},{7,6},{9,8},{10,9},{11,10},{13,12},{... | collective-permute-start | bytes 6344 | tf_op jit(solution)/shard_map/ppermute | solution.py:25
  199.1 11.0 %collective-permute-start.23 = (f32[8,1,66]{1,2,0:T(8,128)S(1)}, f32[8,1,66]{1,2,0:T(8,128)S(1)}, u32[]{:S(2)}, u32[]{:S(2)}) collective-permute-start(f32[8,1,66]{1,2,0:T(8,128)S(1)} %get-tuple-element.22), channel_id=1, source_target_pairs={{0,1},{1,2},{2,3},{4,5},{5,6},{6,7},{8,9},{9,10},{10,11},{12,13},{... | collective-permute-start | bytes 6344 | tf_op jit(solution)/shard_map/ppermute | solution.py:24
  229.5 28.2 %copy-start.4 = (bf16[8,4,8,128]{3,2,1,0:T(8,128)(2,1)S(1)}, bf16[8,4,8,128]{3,2,1,0:T(8,128)(2,1)}, u32[]{:S(2)}) copy-start(bf16[8,4,8,128]{3,2,1,0:T(8,128)(2,1)} %param.8) | copy-start | bytes 196612
  (6 other events, 21.0 us)
Sparse Core Ops, SparseCore 0:
  73.4 33.2 reduce-scatter.6
  233.1 24.5 reduce-scatter.4
